TPU v7x, 256 devices: a whole 4x4x8 slice. The times are simulated.
256 devices in a mesh: grp: 8 (over z_hi, core), mem: 32 (over z_lo, x, y).
Axes of the slice: x: 4, y: 4, z: 8 (z_hi: 4, z_lo: 2; z = z_hi * 2 + z_lo), core: 2. Of those that a mesh axis runs over, the one named last changes fastest.
Arguments:
- spectra: bfloat16 [2048, 2, 16, 512], P(('grp', 'mem')), may hold values from -40 to 40
- partners: int32 [2, 32], replicated, may hold values from 0 to 7, as said below
Outputs:
- correlations: bfloat16 [2048, 2, 256, 513], P(('grp', 'mem'))
Inputs may be any that keep to these rules, and one draw needn't show every extreme that they name: For each member index k the offsets partners[r, k] of the rounds are distinct (offset 0 pairs a block with its own group).
All inputs are finite; a program needn't handle non-finite values.
Results may differ from a plain program's by a relative error of at most 0.0068.
Values may be sent and summed in bfloat16 or wider, within the bound.
No kernel may reach another device: no remote copies, remote signals or barrier semaphores. Data moves between devices by JAX's collectives and lax.ppermute only.
A program may use at most 128 MiB of HBM per device.

v0:
```python
import math
import jax
import jax.numpy as jnp
from jax import lax
from jax.sharding import PartitionSpec as P

SMOOTH = 32


def from_partner(array, axis, distance):
    return lax.ppermute(array, axis, [(i, i ^ 1 << distance) for i in range(lax.axis_size(axis))])


def whiten(spectra, half_width):
    components = spectra.astype(jnp.float32)
    power_sum = components[:, 0] * components[:, 0] + components[:, 1] * components[:, 1]
    bin_count = power_sum.shape[-1]
    positions = jnp.arange(bin_count, dtype=jnp.int32)
    band_matrix = (jnp.abs(positions[:, None] - positions[None, :]) <= half_width).astype(
        jnp.float32
    )
    smooth = jnp.dot(power_sum.reshape(-1, bin_count), band_matrix, precision=lax.Precision.HIGHEST)
    smooth = smooth.reshape(power_sum.shape) / (2 * half_width + 1)
    inv_level = lax.rsqrt(smooth + 1e-05)
    return (components * inv_level[:, None]).astype(jnp.bfloat16)


def lag_table(bin_count):
    centre = bin_count // 2
    frequency = jnp.arange(bin_count, dtype=jnp.int32)[:, None]
    lag_offset = jnp.arange(bin_count + 1, dtype=jnp.int32)[None, :] - centre
    angles = jnp.mod(frequency * lag_offset, 2 * bin_count).astype(jnp.float32) * (
        math.pi / bin_count
    )
    return jnp.stack([jnp.cos(angles), -jnp.sin(angles)], 0).astype(jnp.bfloat16)


def pair_lags(own_block, partner_block, transform):
    factor = math.sqrt(2.0 / (own_block.shape[3] * own_block.shape[2]))
    rotated = jnp.stack([own_block, jnp.stack([own_block[:, 1], -own_block[:, 0]], 1)], 0)
    cross_spectra = jnp.einsum(
        "oicsf,jcsf->ofij", rotated, partner_block, preferred_element_type=jnp.float32
    ).astype(jnp.bfloat16)
    lag_sums = jnp.einsum(
        "ofij,ofl->ijl", cross_spectra, transform, preferred_element_type=jnp.float32
    )
    return (lag_sums * factor).astype(jnp.bfloat16)


def correlate_piece(own_block, transform, received):
    return pair_lags(own_block, received, transform)


def route_shard(payload, offset, levels):
    for level in range(levels):
        swapped = from_partner(payload, "grp", level)
        payload = jnp.where(offset // 2**level % 2 == 1, swapped, payload)
    return payload


def on_device(spectra, partners):
    whitened = whiten(spectra, SMOOTH)
    transform = lag_table(spectra.shape[3])
    rounds = partners.shape[0]
    member_index = lax.axis_index("mem")
    levels = lax.axis_size("grp").bit_length() - 1
    outputs = []
    for round_index in range(rounds):
        own_offset = partners[round_index, member_index]
        source = route_shard(whitened, own_offset, levels)
        outputs.append(
            correlate_piece(whitened, transform, lax.all_gather(source, "mem", axis=0, tiled=True))
        )
    return jnp.stack(outputs, 1)


def solution(mesh):
    placed = (P(("grp", "mem"), None, None, None), P())
    return jax.shard_map(
        on_device,
        mesh=mesh,
        in_specs=placed,
        out_specs=P(("grp", "mem"), None, None, None),
        check_vma=False,
    )
```

profile of v0, /device:TPU:8, one launch (start us, length us, event | category | flops | bytes accessed | tf_op | source)
XLA Modules:
  0.0 450.0 jit_solution(15983893650686171145)
XLA Ops:
  6.5 1.0 convert_element_type.42
  7.6 0.4 fusion.15
  8.0 1.0 multiply_convert_fusion
  9.0 0.1 collective-permute-start
  9.1 1.3 constant_dynamic-slice_fusion.1
  14.2 1.1 broadcast_select_fusion.3
  15.2 3.4 collective-permute-start.1
  19.3 11.9 %collective-permute-done.1 = bf16[8,2,16,512]{3,2,1,0:T(8,128)(2,1)S(1)} collective-permute-done((bf16[8,2,16,512]{3,2,1,0:T(8,128)(2,1)S(1)}, bf16[8,2,16,512]{3,2,1,0:T(8,128)(2,1)S(1)}, u32[]{:S(2)}, u32[]{:S(2)}) %collective-permute-start.1) | collective-permute-done | bytes 262176 | tf_op jit(solution)/shard_map/ppermute | solution.py:11
  31.2 6.6 %collective-permute-start.2 = (bf16[8,2,16,512]{3,2,1,0:T(8,128)(2,1)S(1)}, bf16[8,2,16,512]{3,2,1,0:T(8,128)(2,1)S(1)}, u32[]{:S(2)}, u32[]{:S(2)}) collective-permute-start(bf16[8,2,16,512]{3,2,1,0:T(8,128)(2,1)S(1)} %broadcast_select_fusion.4), channel_id=1, source_target_pairs={{0,128},{32,160},{64,192},{96,224},{128,0},{160,32},{192,64},{224,... | collective-permute-start | bytes 786440 | tf_op jit(solution)/shard_map/ppermute | solution.py:11
  37.9 11.9 %collective-permute-done.2 = bf16[8,2,16,512]{3,2,1,0:T(8,128)(2,1)S(1)} collective-permute-done((bf16[8,2,16,512]{3,2,1,0:T(8,128)(2,1)S(1)}, bf16[8,2,16,512]{3,2,1,0:T(8,128)(2,1)S(1)}, u32[]{:S(2)}, u32[]{:S(2)}) %collective-permute-start.2) | collective-permute-done | bytes 262176 | tf_op jit(solution)/shard_map/ppermute | solution.py:11
  49.7 0.7 broadcast_select_fusion.5
  50.4 0.0 all-gather.3.cloned.1.call-update
  50.5 0.0 all-gather.5.cloned.1.call-start
  50.5 0.1 collective-permute-start.3
  51.2 10.8 %collective-permute-done.3 = bf16[8,2,16,512]{3,2,1,0:T(8,128)(2,1)S(1)} collective-permute-done((bf16[8,2,16,512]{3,2,1,0:T(8,128)(2,1)S(1)}, bf16[8,2,16,512]{3,2,1,0:T(8,128)(2,1)S(1)}, u32[]{:S(2)}, u32[]{:S(2)}) %collective-permute-start.3) | collective-permute-done | bytes 262176 | tf_op jit(solution)/shard_map/ppermute | solution.py:11
  62.1 5.1 %collective-permute-start.4 = (bf16[8,2,16,512]{3,2,1,0:T(8,128)(2,1)S(1)}, bf16[8,2,16,512]{3,2,1,0:T(8,128)(2,1)S(1)}, u32[]{:S(2)}, u32[]{:S(2)}) collective-permute-start(bf16[8,2,16,512]{3,2,1,0:T(8,128)(2,1)S(1)} %broadcast_select_fusion.1), channel_id=1, source_target_pairs={{0,128},{32,160},{64,192},{96,224},{128,0},{160,32},{192,64},{224,... | collective-permute-start | bytes 786440 | tf_op jit(solution)/shard_map/ppermute | solution.py:11
  67.2 11.3 %collective-permute-done.4 = bf16[8,2,16,512]{3,2,1,0:T(8,128)(2,1)S(1)} collective-permute-done((bf16[8,2,16,512]{3,2,1,0:T(8,128)(2,1)S(1)}, bf16[8,2,16,512]{3,2,1,0:T(8,128)(2,1)S(1)}, u32[]{:S(2)}, u32[]{:S(2)}) %collective-permute-start.4) | collective-permute-done | bytes 262176 | tf_op jit(solution)/shard_map/ppermute | solution.py:11
  78.5 0.7 broadcast_select_fusion.2
  79.3 0.1 fusion.38
  79.4 0.1 pad_maximum_fusion.1
  79.4 6.4 %copy.6 = bf16[2,8,2,16,512]{3,1,2,0,4:T(8,128)(2,1)} copy(bf16[2,8,2,16,512]{4,3,2,1,0:T(8,128)(2,1)S(1)} %pad_maximum_fusion.1) | data formatting | bytes 1048576 | tf_op jit(solution)/shard_map/stack | solution.py:40
  85.9 4.7 %cosine_convert_fusion = (bf16[1,512,513]{1,2,0:T(8,128)(2,1)S(1)}, bf16[1,512,513]{1,2,0:T(8,128)(2,1)S(1)}) fusion(s32[513]{0:T(1024)S(1)} %iota_add_fusion), kind=kLoop, calls=%fused_computation.24 | loop fusion | flops 4465152 | bytes 1052676 | tf_op jit(solution)/shard_map/convert
  90.6 132.0 %all-gather.3.cloned.1.call-done = bf16[256,2,16,512]{3,2,1,0:T(8,128)(2,1)} async-done(((bf16[8,2,16,512]{3,2,1,0:T(8,128)(2,1)}), bf16[256,2,16,512]{3,2,1,0:T(8,128)(2,1)}) %all-gather.3.cloned.1.call-update) | async-done | bytes 8388624 | tf_op jit(solution)/shard_map/all_gather | solution.py:72
  222.6 15.9 %copy.5 = bf16[256,2,16,512,1]{0,2,1,4,3:T(8,128)(2,1)} copy(bf16[256,2,16,512,1]{3,2,1,0,4:T(8,128)(2,1)} %bitcast.64) | data formatting | bytes 16777216 | tf_op jit(solution)/shard_map/all_gather | solution.py:72
  238.6 158.3 %all-gather.5.cloned.1.call-done = bf16[256,2,16,512]{3,2,1,0:T(8,128)(2,1)} async-done(((bf16[8,2,16,512]{3,2,1,0:T(8,128)(2,1)}), bf16[256,2,16,512]{3,2,1,0:T(8,128)(2,1)}) %all-gather.5.cloned.1.call-update) | async-done | bytes 8388624 | tf_op jit(solution)/shard_map/all_gather | solution.py:72
  396.9 16.0 %copy.9 = bf16[256,2,16,512,1]{0,2,1,4,3:T(8,128)(2,1)} copy(bf16[256,2,16,512,1]{3,2,1,0,4:T(8,128)(2,1)} %bitcast.65) | data formatting | bytes 16777216 | tf_op jit(solution)/shard_map/all_gather | solution.py:72
  412.9 8.0 %fusion.32 = bf16[512,256,2,8,1]{1,3,4,2,0:T(8,128)(2,1)} fusion(bf16[256,2,16,512,1]{0,2,1,4,3:T(8,128)(2,1)} %copy.5, bf16[2,8,2,16,512]{3,1,2,0,4:T(8,128)(2,1)} %copy.6), kind=kOutput, calls=%fused_computation.52 | convolution fusion | flops 134217728 | bytes 13107200 | tf_op jit(solution)/shard_map/oicsf,jcsf->ofij/dot_general | solution.py:41
  420.8 7.9 %fusion.33 = bf16[512,256,2,8,1]{1,3,4,2,0:T(8,128)(2,1)} fusion(bf16[256,2,16,512,1]{0,2,1,4,3:T(8,128)(2,1)} %copy.9, bf16[2,8,2,16,512]{3,1,2,0,4:T(8,128)(2,1)} %copy.6), kind=kOutput, calls=%fused_computation.53 | convolution fusion | flops 134217728 | bytes 13107200 | tf_op jit(solution)/shard_map/oicsf,jcsf->ofij/dot_general | solution.py:41
  428.8 5.0 %fusion.8 = bf16[8,1,256,513]{2,3,0,1:T(8,128)(2,1)S(1)} fusion(bf16[512,256,2,8,1]{1,3,4,2,0:T(8,128)(2,1)} %fusion.32, bf16[1,512,513]{1,2,0:T(8,128)(2,1)S(1)} %get-tuple-element.10, bf16[1,512,513]{1,2,0:T(8,128)(2,1)S(1)} %get-tuple-element.9), kind=kOutput, calls=%fused_computation.11 | convolution fusion | flops 2154304512 | bytes 7346176 | tf_op jit(solution)/shard_map/ofij,ofl->ijl/dot_general | solution.py:44
  433.8 2.7 fusion.9
  436.5 0.4 pad_maximum_fusion
  436.8 6.3 %copy.4 = bf16[8,2,256,513]{2,1,3,0:T(2,128)(2,1)} copy(bf16[8,2,256,513]{2,3,0,1:T(8,128)(2,1)S(1)} %pad_maximum_fusion) | data formatting | bytes 8404992 | tf_op jit(solution)/shard_map/stack | solution.py:74
  (12 shorter events, 0.1 us)
Async XLA Ops:
  6.5 216.1 %all-gather.3.cloned.1.call-start = ((), (), s32[]{:S(2)}) async-start(), calls=%async_computation | async-start | bytes 8650752 | tf_op jit(solution)/shard_map/all_gather | solution.py:72
  7.5 71.8 %copy-start = (bf16[8,2,16,512]{3,2,1,0:T(8,128)(2,1)S(1)}, bf16[8,2,16,512]{3,2,1,0:T(8,128)(2,1)}, u32[]{:S(2)}) copy-start(bf16[8,2,16,512]{3,2,1,0:T(8,128)(2,1)} %param.2) | copy-start | bytes 786436
  9.0 5.1 %collective-permute-start = (bf16[8,2,16,512]{3,2,1,0:T(8,128)(2,1)S(1)}, bf16[8,2,16,512]{3,2,1,0:T(8,128)(2,1)S(1)}, u32[]{:S(2)}, u32[]{:S(2)}) collective-permute-start(bf16[8,2,16,512]{3,2,1,0:T(8,128)(2,1)S(1)} %multiply_convert_fusion), channel_id=1, source_target_pairs={{0,32},{32,0},{64,96},{96,64},{128,160},{160,128},{192,224},{224,1... | collective-permute-start | bytes 786440 | tf_op jit(solution)/shard_map/ppermute | solution.py:11
  15.2 15.9 %collective-permute-start.1 = (bf16[8,2,16,512]{3,2,1,0:T(8,128)(2,1)S(1)}, bf16[8,2,16,512]{3,2,1,0:T(8,128)(2,1)S(1)}, u32[]{:S(2)}, u32[]{:S(2)}) collective-permute-start(bf16[8,2,16,512]{3,2,1,0:T(8,128)(2,1)S(1)} %get-tuple-element.5), channel_id=1, source_target_pairs={{0,64},{32,96},{64,0},{96,32},{128,192},{160,224},{192,128},{224,1... | collective-permute-start | bytes 786440 | tf_op jit(solution)/shard_map/ppermute | solution.py:11
  31.2 18.5 %collective-permute-start.2 = (bf16[8,2,16,512]{3,2,1,0:T(8,128)(2,1)S(1)}, bf16[8,2,16,512]{3,2,1,0:T(8,128)(2,1)S(1)}, u32[]{:S(2)}, u32[]{:S(2)}) collective-permute-start(bf16[8,2,16,512]{3,2,1,0:T(8,128)(2,1)S(1)} %broadcast_select_fusion.4), channel_id=1, source_target_pairs={{0,128},{32,160},{64,192},{96,224},{128,0},{160,32},{192,64},{224,... | collective-permute-start | bytes 786440 | tf_op jit(solution)/shard_map/ppermute | solution.py:11
  50.5 346.4 %all-gather.5.cloned.1.call-start = ((), (), s32[]{:S(2)}) async-start(), calls=%async_computation.1 | async-start | bytes 8650752 | tf_op jit(solution)/shard_map/all_gather | solution.py:72
  50.5 11.5 %collective-permute-start.3 = (bf16[8,2,16,512]{3,2,1,0:T(8,128)(2,1)S(1)}, bf16[8,2,16,512]{3,2,1,0:T(8,128)(2,1)S(1)}, u32[]{:S(2)}, u32[]{:S(2)}) collective-permute-start(bf16[8,2,16,512]{3,2,1,0:T(8,128)(2,1)S(1)} %get-tuple-element.6), channel_id=1, source_target_pairs={{0,64},{32,96},{64,0},{96,32},{128,192},{160,224},{192,128},{224,1... | collective-permute-start | bytes 786440 | tf_op jit(solution)/shard_map/ppermute | solution.py:11
  62.1 16.4 %collective-permute-start.4 = (bf16[8,2,16,512]{3,2,1,0:T(8,128)(2,1)S(1)}, bf16[8,2,16,512]{3,2,1,0:T(8,128)(2,1)S(1)}, u32[]{:S(2)}, u32[]{:S(2)}) collective-permute-start(bf16[8,2,16,512]{3,2,1,0:T(8,128)(2,1)S(1)} %broadcast_select_fusion.1), channel_id=1, source_target_pairs={{0,128},{32,160},{64,192},{96,224},{128,0},{160,32},{192,64},{224,... | collective-permute-start | bytes 786440 | tf_op jit(solution)/shard_map/ppermute | solution.py:11
  428.8 5.0 %copy-start.1 = (bf16[512,256,2,8,1]{1,3,4,2,0:T(8,128)(2,1)S(1)}, bf16[512,256,2,8,1]{1,3,4,2,0:T(8,128)(2,1)}, u32[]{:S(2)}) copy-start(bf16[512,256,2,8,1]{1,3,4,2,0:T(8,128)(2,1)} %fusion.33) | copy-start | bytes 12582916
Sparse Core Ops, SparseCore 0:
  50.6 171.9 all-gather.2
  224.4 172.4 all-gather.4
where the time goes:
time: 451 us; the launch traced here: 450 us
  waiting for transfers between devices  336 us (75%)
  local copies, waits for them, and re-layouts  46 us (10%)
  matrix products  24 us (5%)
  between operations  18.5 us (4%)
  starting transfers between devices  15.3 us (3%)
  other arithmetic  9.86 us (2%)
    all_gather x2, waiting for transfers between devices, on_device(): lax.all_gather(source, 'mem', axis=0, tiled=True)  290 us
    ppermute x5, waiting for transfers between devices, from_partner(): lax.ppermute(array, axis, [(i, i ^ 1 << distance) for i in range(lax.axis...  45.9 us
    all_gather x2, local copies, waits for them, and re-layouts, on_device(): lax.all_gather(source, 'mem', axis=0, tiled=True)  31.9 us
    dot_general x2, matrix products, pair_lags(): jnp.einsum('oicsf,jcsf->ofij', rotated, partner_block, preferred_element_...  15.9 us
    ppermute x5, starting transfers between devices, from_partner(): lax.ppermute(array, axis, [(i, i ^ 1 << distance) for i in range(lax.axis...  15.3 us
  transfers between devices with their start and end apart: 7, of which 6 were waited for; matrix products, arithmetic and copies ran while one was open for 7% of the time, Pallas kernels for 0%

commit v1 on v0

--- a/solution.py
+++ b/solution.py
@@ -69,7 +69,13 @@
         own_offset = partners[round_index, member_index]
         source = route_shard(whitened, own_offset, levels)
         outputs.append(
-            correlate_piece(whitened, transform, lax.all_gather(source, "mem", axis=0, tiled=True))
+            correlate_piece(
+                whitened,
+                transform,
+                jnp.concatenate(
+                    lax.all_to_all(jnp.stack([source] * lax.axis_size("mem")), "mem", 0, 0), axis=0
+                ),
+            )
         )
     return jnp.stack(outputs, 1)
 

time: 451 us -> 379 us (0.84)
  waiting for transfers between devices: 336 us -> 222 us
  starting transfers between devices: 15.3 us -> 60.1 us
  between operations: 18.5 us -> 5.39 us
  local copies, waits for them, and re-layouts: 46 us -> 54.7 us
    all_gather x2 -> x0, waiting for transfers between devices: 290 us -> none  [on_device(): lax.all_gather(source, 'mem', axis=0, tiled=True)]
    all_to_all x0 -> x2, waiting for transfers between devices: none -> 92.7 us  [on_device(): lax.all_to_all(jnp.stack([source] * lax.axis_size('mem')), 'mem', 0, 0)]
    ppermute x5, waiting for transfers between devices: 45.9 us -> 129 us  [from_partner(): lax.ppermute(array, axis, [(i, i ^ 1 << distance) for i in range(lax.axis...]
    all_gather x2 -> x0, local copies, waits for them, and re-layouts: 31.9 us -> none  [on_device(): lax.all_gather(source, 'mem', axis=0, tiled=True)]
    reshape x0 -> x2, local copies, waits for them, and re-layouts: none -> 31.9 us  [on_device(): jnp.concatenate(lax.all_to_all(jnp.stack([source] * lax.axis_size('mem'))...]
    all_to_all x0 -> x2, starting transfers between devices: none -> 28.6 us  [on_device(): lax.all_to_all(jnp.stack([source] * lax.axis_size('mem')), 'mem', 0, 0)]
    ppermute x5, starting transfers between devices: 15.3 us -> 31.5 us  [from_partner(): lax.ppermute(array, axis, [(i, i ^ 1 << distance) for i in range(lax.axis...]
    another operation x0 -> x2, local copies, waits for them, and re-layouts: none -> 8.6 us  [on_device(): jnp.stack([source] * lax.axis_size('mem'))]
  transfers between devices with their start and end apart: 7 -> 7, of which waited for: 6 -> 5; matrix products, arithmetic and copies ran while one was open for 7% -> 8% of each run, Pallas kernels for 0% -> 0%
where the time goes in v1:
time: 379 us; the launch traced here: 375 us
  waiting for transfers between devices  222 us (59%)
  starting transfers between devices  60.1 us (16%)
  local copies, waits for them, and re-layouts  54.7 us (14%)
  matrix products  24 us (6%)
  other arithmetic  8.45 us (2%)
  between operations  5.39 us (1%)
    ppermute x5, waiting for transfers between devices, from_partner(): lax.ppermute(array, axis, [(i, i ^ 1 << distance) for i in range(lax.axis...  129 us
    all_to_all x2, waiting for transfers between devices, on_device(): lax.all_to_all(jnp.stack([source] * lax.axis_size('mem')), 'mem', 0, 0)  92.7 us
    reshape x2, local copies, waits for them, and re-layouts, on_device(): jnp.concatenate(lax.all_to_all(jnp.stack([source] * lax.axis_size('mem'))...  31.9 us
    ppermute x5, starting transfers between devices, from_partner(): lax.ppermute(array, axis, [(i, i ^ 1 << distance) for i in range(lax.axis...  31.5 us
    all_to_all x2, starting transfers between devices, on_device(): lax.all_to_all(jnp.stack([source] * lax.axis_size('mem')), 'mem', 0, 0)  28.6 us
    dot_general x2, matrix products, pair_lags(): jnp.einsum('oicsf,jcsf->ofij', rotated, partner_block, preferred_element_...  15.9 us
    another operation x2, local copies, waits for them, and re-layouts, on_device(): jnp.stack([source] * lax.axis_size('mem'))  8.6 us
    dot_general x2, matrix products, pair_lags(): jnp.einsum('ofij,ofl->ijl', cross_spectra, transform, preferred_element_t...  7.68 us
  transfers between devices with their start and end apart: 7, of which 5 were waited for; matrix products, arithmetic and copies ran while one was open for 8% of the time, Pallas kernels for 0%

profile of v1, /device:TPU:8, one launch (start us, length us, event | category | flops | bytes accessed | tf_op | source)
XLA Modules:
  0.0 374.8 jit_solution(12017292306454810374)
XLA Ops:
  0.0 1.0 convert_element_type.42
  1.0 0.5 fusion.15
  1.5 1.0 multiply_convert_fusion
  2.5 0.1 collective-permute-start
  2.6 1.4 constant_dynamic-slice_fusion.1
  7.8 0.0 collective-permute-done
  7.8 1.1 broadcast_select_fusion.3
  8.9 3.4 collective-permute-start.3
  12.9 11.9 %collective-permute-done.3 = bf16[8,2,16,512]{3,2,1,0:T(8,128)(2,1)S(1)} collective-permute-done((bf16[8,2,16,512]{3,2,1,0:T(8,128)(2,1)S(1)}, bf16[8,2,16,512]{3,2,1,0:T(8,128)(2,1)S(1)}, u32[]{:S(2)}, u32[]{:S(2)}) %collective-permute-start.3) | collective-permute-done | bytes 262176 | tf_op jit(solution)/shard_map/ppermute | solution.py:11
  24.9 6.6 %collective-permute-start.4 = (bf16[8,2,16,512]{3,2,1,0:T(8,128)(2,1)S(1)}, bf16[8,2,16,512]{3,2,1,0:T(8,128)(2,1)S(1)}, u32[]{:S(2)}, u32[]{:S(2)}) collective-permute-start(bf16[8,2,16,512]{3,2,1,0:T(8,128)(2,1)S(1)} %broadcast_select_fusion.1), channel_id=1, source_target_pairs={{0,128},{32,160},{64,192},{96,224},{128,0},{160,32},{192,64},{224,... | collective-permute-start | bytes 786440 | tf_op jit(solution)/shard_map/ppermute | solution.py:11
  31.5 11.9 %collective-permute-done.4 = bf16[8,2,16,512]{3,2,1,0:T(8,128)(2,1)S(1)} collective-permute-done((bf16[8,2,16,512]{3,2,1,0:T(8,128)(2,1)S(1)}, bf16[8,2,16,512]{3,2,1,0:T(8,128)(2,1)S(1)}, u32[]{:S(2)}, u32[]{:S(2)}) %collective-permute-start.4) | collective-permute-done | bytes 262176 | tf_op jit(solution)/shard_map/ppermute | solution.py:11
  43.4 4.3 %stack.28 = bf16[32,8,2,16,512]{4,3,2,1,0:T(8,128)(2,1)} broadcast(bf16[8,2,16,512]{3,2,1,0:T(8,128)(2,1)S(1)} %broadcast_select_fusion.2), dimensions={1,2,3,4} | broadcast | bytes 8650752 | tf_op jit(solution)/shard_map/stack | solution.py:76
  47.7 7.6 %all-to-all-start.1 = ((bf16[32,8,2,16,512]{4,3,2,1,0:T(8,128)(2,1)}), bf16[32,8,2,16,512]{4,3,2,1,0:T(8,128)(2,1)}, u32[]{:S(2)}, u32[]{:S(2)}) async-start(bf16[32,8,2,16,512]{4,3,2,1,0:T(8,128)(2,1)} %stack.28), calls=%async_computation.1 | async-start | bytes 16777216 | tf_op jit(solution)/shard_map/all_to_all | solution.py:76
  55.3 3.1 collective-permute-start.1
  59.1 101.0 %collective-permute-done.1 = bf16[8,2,16,512]{3,2,1,0:T(8,128)(2,1)S(1)} collective-permute-done((bf16[8,2,16,512]{3,2,1,0:T(8,128)(2,1)S(1)}, bf16[8,2,16,512]{3,2,1,0:T(8,128)(2,1)S(1)}, u32[]{:S(2)}, u32[]{:S(2)}) %collective-permute-start.1) | collective-permute-done | bytes 262176 | tf_op jit(solution)/shard_map/ppermute | solution.py:11
  160.1 18.3 %collective-permute-start.2 = (bf16[8,2,16,512]{3,2,1,0:T(8,128)(2,1)S(1)}, bf16[8,2,16,512]{3,2,1,0:T(8,128)(2,1)S(1)}, u32[]{:S(2)}, u32[]{:S(2)}) collective-permute-start(bf16[8,2,16,512]{3,2,1,0:T(8,128)(2,1)S(1)} %broadcast_select_fusion.4), channel_id=1, source_target_pairs={{0,128},{32,160},{64,192},{96,224},{128,0},{160,32},{192,64},{224,... | collective-permute-start | bytes 786440 | tf_op jit(solution)/shard_map/ppermute | solution.py:11
  178.5 4.7 %collective-permute-done.2 = bf16[8,2,16,512]{3,2,1,0:T(8,128)(2,1)S(1)} collective-permute-done((bf16[8,2,16,512]{3,2,1,0:T(8,128)(2,1)S(1)}, bf16[8,2,16,512]{3,2,1,0:T(8,128)(2,1)S(1)}, u32[]{:S(2)}, u32[]{:S(2)}) %collective-permute-start.2) | collective-permute-done | bytes 262176 | tf_op jit(solution)/shard_map/ppermute | solution.py:11
  183.2 4.3 %stack.21 = bf16[32,8,2,16,512]{4,3,2,1,0:T(8,128)(2,1)} broadcast(bf16[8,2,16,512]{3,2,1,0:T(8,128)(2,1)S(1)} %broadcast_select_fusion.5), dimensions={1,2,3,4} | broadcast | bytes 8650752 | tf_op jit(solution)/shard_map/stack | solution.py:76
  187.5 21.0 %all-to-all-start = ((bf16[32,8,2,16,512]{4,3,2,1,0:T(8,128)(2,1)}), bf16[32,8,2,16,512]{4,3,2,1,0:T(8,128)(2,1)}, u32[]{:S(2)}, u32[]{:S(2)}) async-start(bf16[32,8,2,16,512]{4,3,2,1,0:T(8,128)(2,1)} %stack.21), calls=%async_computation | async-start | bytes 16777216 | tf_op jit(solution)/shard_map/all_to_all | solution.py:76
  208.6 0.1 fusion.38
  208.7 0.1 pad_maximum_fusion.1
  208.7 6.4 %copy.5 = bf16[2,8,2,16,512]{3,1,2,0,4:T(8,128)(2,1)} copy(bf16[2,8,2,16,512]{4,3,2,1,0:T(8,128)(2,1)S(1)} %pad_maximum_fusion.1) | data formatting | bytes 1048576 | tf_op jit(solution)/shard_map/stack | solution.py:40
  215.2 4.7 %cosine_convert_fusion = (bf16[1,512,513]{1,2,0:T(8,128)(2,1)S(1)}, bf16[1,512,513]{1,2,0:T(8,128)(2,1)S(1)}) fusion(s32[513]{0:T(1024)S(1)} %iota_add_fusion), kind=kLoop, calls=%fused_computation.24 | loop fusion | flops 4465152 | bytes 1052676 | tf_op jit(solution)/shard_map/convert
  219.9 16.0 %copy.8 = bf16[256,2,16,512,1]{0,2,1,4,3:T(8,128)(2,1)} copy(bf16[256,2,16,512,1]{3,2,1,0,4:T(8,128)(2,1)} %bitcast.15) | data formatting | bytes 16777216 | tf_op jit(solution)/shard_map/reshape | solution.py:75
  235.9 92.7 %all-to-all-done = bf16[32,8,2,16,512]{4,3,2,1,0:T(8,128)(2,1)} async-done(((bf16[32,8,2,16,512]{4,3,2,1,0:T(8,128)(2,1)}), bf16[32,8,2,16,512]{4,3,2,1,0:T(8,128)(2,1)}, u32[]{:S(2)}, u32[]{:S(2)}) %all-to-all-start) | async-done | bytes 8388640 | tf_op jit(solution)/shard_map/all_to_all | solution.py:76
  328.6 15.9 %copy.4 = bf16[256,2,16,512,1]{0,2,1,4,3:T(8,128)(2,1)} copy(bf16[256,2,16,512,1]{3,2,1,0,4:T(8,128)(2,1)} %bitcast.4) | data formatting | bytes 16777216 | tf_op jit(solution)/shard_map/reshape | solution.py:75
  344.5 8.0 %fusion.33 = bf16[512,256,2,8,1]{1,3,4,2,0:T(8,128)(2,1)} fusion(bf16[256,2,16,512,1]{0,2,1,4,3:T(8,128)(2,1)} %copy.8, bf16[2,8,2,16,512]{3,1,2,0,4:T(8,128)(2,1)} %copy.5), kind=kOutput, calls=%fused_computation.53 | convolution fusion | flops 134217728 | bytes 13107200 | tf_op jit(solution)/shard_map/oicsf,jcsf->ofij/dot_general | solution.py:41
  352.4 7.9 %fusion.32 = bf16[512,256,2,8,1]{1,3,4,2,0:T(8,128)(2,1)} fusion(bf16[256,2,16,512,1]{0,2,1,4,3:T(8,128)(2,1)} %copy.4, bf16[2,8,2,16,512]{3,1,2,0,4:T(8,128)(2,1)} %copy.5), kind=kOutput, calls=%fused_computation.52 | convolution fusion | flops 134217728 | bytes 13107200 | tf_op jit(solution)/shard_map/oicsf,jcsf->ofij/dot_general | solution.py:41
  360.4 5.0 %fusion.9 = bf16[8,1,256,513]{2,3,0,1:T(8,128)(2,1)S(1)} fusion(bf16[512,256,2,8,1]{1,3,4,2,0:T(8,128)(2,1)} %fusion.33, bf16[1,512,513]{1,2,0:T(8,128)(2,1)S(1)} %get-tuple-element.10, bf16[1,512,513]{1,2,0:T(8,128)(2,1)S(1)} %get-tuple-element.9), kind=kOutput, calls=%fused_computation.12 | convolution fusion | flops 2154304512 | bytes 7346176 | tf_op jit(solution)/shard_map/ofij,ofl->ijl/dot_general | solution.py:44
  365.4 2.7 fusion.8
  368.1 0.4 pad_maximum_fusion
  368.4 6.3 %copy.3 = bf16[8,2,256,513]{2,1,3,0:T(2,128)(2,1)} copy(bf16[8,2,256,513]{2,3,0,1:T(8,128)(2,1)S(1)} %pad_maximum_fusion) | data formatting | bytes 8404992 | tf_op jit(solution)/shard_map/stack | solution.py:80
  (12 shorter events, 0.2 us)
Async XLA Ops:
  2.5 5.3 %collective-permute-start = (bf16[8,2,16,512]{3,2,1,0:T(8,128)(2,1)S(1)}, bf16[8,2,16,512]{3,2,1,0:T(8,128)(2,1)S(1)}, u32[]{:S(2)}, u32[]{:S(2)}) collective-permute-start(bf16[8,2,16,512]{3,2,1,0:T(8,128)(2,1)S(1)} %multiply_convert_fusion), channel_id=1, source_target_pairs={{0,32},{32,0},{64,96},{96,64},{128,160},{160,128},{192,224},{224,1... | collective-permute-start | bytes 786440 | tf_op jit(solution)/shard_map/ppermute | solution.py:11
  8.9 15.9 %collective-permute-start.3 = (bf16[8,2,16,512]{3,2,1,0:T(8,128)(2,1)S(1)}, bf16[8,2,16,512]{3,2,1,0:T(8,128)(2,1)S(1)}, u32[]{:S(2)}, u32[]{:S(2)}) collective-permute-start(bf16[8,2,16,512]{3,2,1,0:T(8,128)(2,1)S(1)} %get-tuple-element.6), channel_id=1, source_target_pairs={{0,64},{32,96},{64,0},{96,32},{128,192},{160,224},{192,128},{224,1... | collective-permute-start | bytes 786440 | tf_op jit(solution)/shard_map/ppermute | solution.py:11
  24.9 18.5 %collective-permute-start.4 = (bf16[8,2,16,512]{3,2,1,0:T(8,128)(2,1)S(1)}, bf16[8,2,16,512]{3,2,1,0:T(8,128)(2,1)S(1)}, u32[]{:S(2)}, u32[]{:S(2)}) collective-permute-start(bf16[8,2,16,512]{3,2,1,0:T(8,128)(2,1)S(1)} %broadcast_select_fusion.1), channel_id=1, source_target_pairs={{0,128},{32,160},{64,192},{96,224},{128,0},{160,32},{192,64},{224,... | collective-permute-start | bytes 786440 | tf_op jit(solution)/shard_map/ppermute | solution.py:11
  47.7 135.4 %all-to-all-start.1 = ((bf16[32,8,2,16,512]{4,3,2,1,0:T(8,128)(2,1)}), bf16[32,8,2,16,512]{4,3,2,1,0:T(8,128)(2,1)}, u32[]{:S(2)}, u32[]{:S(2)}) async-start(bf16[32,8,2,16,512]{4,3,2,1,0:T(8,128)(2,1)} %stack.28), calls=%async_computation.1 | async-start | bytes 16777216 | tf_op jit(solution)/shard_map/all_to_all | solution.py:76
  55.3 104.8 %collective-permute-start.1 = (bf16[8,2,16,512]{3,2,1,0:T(8,128)(2,1)S(1)}, bf16[8,2,16,512]{3,2,1,0:T(8,128)(2,1)S(1)}, u32[]{:S(2)}, u32[]{:S(2)}) collective-permute-start(bf16[8,2,16,512]{3,2,1,0:T(8,128)(2,1)S(1)} %get-tuple-element.5), channel_id=1, source_target_pairs={{0,64},{32,96},{64,0},{96,32},{128,192},{160,224},{192,128},{224,1... | collective-permute-start | bytes 786440 | tf_op jit(solution)/shard_map/ppermute | solution.py:11
  160.1 23.0 %collective-permute-start.2 = (bf16[8,2,16,512]{3,2,1,0:T(8,128)(2,1)S(1)}, bf16[8,2,16,512]{3,2,1,0:T(8,128)(2,1)S(1)}, u32[]{:S(2)}, u32[]{:S(2)}) collective-permute-start(bf16[8,2,16,512]{3,2,1,0:T(8,128)(2,1)S(1)} %broadcast_select_fusion.4), channel_id=1, source_target_pairs={{0,128},{32,160},{64,192},{96,224},{128,0},{160,32},{192,64},{224,... | collective-permute-start | bytes 786440 | tf_op jit(solution)/shard_map/ppermute | solution.py:11
  187.5 21.1 %copy-start = (bf16[8,2,16,512]{3,2,1,0:T(8,128)(2,1)S(1)}, bf16[8,2,16,512]{3,2,1,0:T(8,128)(2,1)}, u32[]{:S(2)}) copy-start(bf16[8,2,16,512]{3,2,1,0:T(8,128)(2,1)} %param.2) | copy-start | bytes 786436
  187.5 141.1 %all-to-all-start = ((bf16[32,8,2,16,512]{4,3,2,1,0:T(8,128)(2,1)}), bf16[32,8,2,16,512]{4,3,2,1,0:T(8,128)(2,1)}, u32[]{:S(2)}, u32[]{:S(2)}) async-start(bf16[32,8,2,16,512]{4,3,2,1,0:T(8,128)(2,1)} %stack.21), calls=%async_computation | async-start | bytes 16777216 | tf_op jit(solution)/shard_map/all_to_all | solution.py:76
  360.4 5.0 %copy-start.1 = (bf16[512,256,2,8,1]{1,3,4,2,0:T(8,128)(2,1)S(1)}, bf16[512,256,2,8,1]{1,3,4,2,0:T(8,128)(2,1)}, u32[]{:S(2)}) copy-start(bf16[512,256,2,8,1]{1,3,4,2,0:T(8,128)(2,1)} %fusion.32) | copy-start | bytes 12582916
